TPU v7x, 256 devices: a whole 4x4x8 slice. The times are simulated.
256 devices in a mesh: row: 8 (over z), col: 32 (over x, y, core).
Axes of the slice: x: 4, y: 4, z: 8, core: 2. Of those that a mesh axis runs over, the one named last changes fastest.
Arguments:
- latitude: bfloat16 [16384, 256], P(('row', 'col')), may hold values from -4 to 4
- longitude: bfloat16 [16384, 512], P(('row', 'col')), may hold values from -4 to 4
- weight: bfloat16 [16384], P(('row', 'col')), may hold values from 0.29882812 to 3
- harmonic_index: int32 [2, 24576], P(None, 'col'), may hold values from 0 to 511, as said below
Outputs:
- coefficients: float32 [512, 24576], P(None, 'col')
- residual: float32 [16384, 24576], P('row', 'col')
Inputs may be any that keep to these rules, and one draw needn't show every extreme that they name: The pairs (harmonic_index[0, j], harmonic_index[1, j]) are distinct over all 24576 columns; row 0 is below 256, and harmonic_index[1, j] // 2 never exceeds harmonic_index[0, j].
All inputs are finite; a program needn't handle non-finite values.
Results may differ from a plain program's by a relative error of at most 0.0003.
Values may be sent and summed in bfloat16 or wider, within the bound.
No kernel may reach another device: no remote copies, remote signals or barrier semaphores. Data moves between devices by JAX's collectives and lax.ppermute only.
A program may use at most 128 MiB of HBM per device.

v0:
```python
import math
import jax
import jax.numpy as jnp
from jax import lax
from jax.sharding import PartitionSpec as P

PANEL = 256


def in_one_piece(arrays, axis, dim, along):
    widths = [math.prod(a.shape[along:]) for a in arrays]
    both = jnp.concatenate(
        [a.reshape(*a.shape[:along], w) for a, w in zip(arrays, widths)], axis=along
    )
    result = lax.all_gather(both, axis, axis=dim, tiled=True)
    tiles = jnp.split(result, [sum(widths[:k]) for k in range(1, len(widths))], axis=along)
    return tuple(
        (b.reshape(*result.shape[:along], *a.shape[along:]) for a, b in zip(arrays, tiles))
    )


def picked(array, axis, root):
    return lax.dynamic_index_in_dim(lax.all_gather(array, axis), root, 0, keepdims=False)


def synthesize(latitude, longitude, weight, column_index):
    degree_hot = (
        column_index[0][None, :] == jnp.arange(latitude.shape[1], dtype=jnp.int32)[:, None]
    ).astype(jnp.bfloat16)
    order_hot = (
        column_index[1][None, :] == jnp.arange(longitude.shape[1], dtype=jnp.int32)[:, None]
    ).astype(jnp.bfloat16)
    picked_degree = jnp.dot(latitude, degree_hot, preferred_element_type=jnp.float32)
    picked_order = jnp.dot(longitude, order_hot, preferred_element_type=jnp.float32)
    return weight.astype(jnp.float32)[:, None] * picked_degree * picked_order


def orthonormal(panel_cols, gram_sum):
    lower_factor = jnp.linalg.cholesky(gram_sum)
    return lax.linalg.triangular_solve(lower_factor, panel_cols.T, left_side=True, lower=True)


def remove_span(design, basis_t, top_rows):
    return design - jnp.dot(
        basis_t.T, top_rows, precision=lax.Precision.HIGHEST, preferred_element_type=jnp.float32
    )


def shards(latitude, longitude, weight, harmonic_index):
    tables = in_one_piece((latitude, longitude, weight), "col", 0, 1)
    lead_index = picked(harmonic_index[:, : 2 * PANEL], "col", 0)
    lead_cols = synthesize(tables[0], tables[1], tables[2], lead_index)
    design = synthesize(tables[0], tables[1], tables[2], harmonic_index)
    local_gram = jnp.dot(
        lead_cols.T, lead_cols, precision=lax.Precision.HIGHEST, preferred_element_type=jnp.float32
    )
    gram_sum = lax.psum(local_gram, "row")
    basis_t = orthonormal(lead_cols, gram_sum)
    local_rows = jnp.dot(
        basis_t, design, precision=lax.Precision.HIGHEST, preferred_element_type=jnp.float32
    )
    coefficients = lax.psum(local_rows, "row")
    residual = remove_span(design, basis_t, coefficients)
    return (coefficients, residual)


def solution(mesh):
    return jax.shard_map(
        shards,
        mesh=mesh,
        in_specs=(
            P(("row", "col"), None),
            P(("row", "col"), None),
            P(("row", "col")),
            P(None, "col"),
        ),
        out_specs=(P(None, "col"), P("row", "col")),
        check_vma=False,
    )
```

profile of v0, /device:TPU:2, one launch (start us, length us, event | category | flops | bytes accessed | tf_op | source)
XLA Modules:
  0.0 433.0 jit_solution(3629395771598168058)
XLA Ops:
  8.0 1.5 pad_maximum_fusion.3
  10.2 24.6 %all-gather.1 = s32[32,2,512]{2,1,0:T(2,128)S(1)} all-gather(s32[1,2,512]{2,1,0:T(2,128)S(1)} %slice_bitcast_fusion.8), channel_id=2, replica_groups=mesh['row'=8,'col'=32] {'col'}, dimensions={0}, use_global_device_ids=true | all-gather | bytes 135168 | tf_op jit(solution)/shard_map/all_gather | solution.py:23
  35.6 28.7 %all-gather.4.cloned.1.call-done = bf16[2048,769]{1,0:T(8,128)(2,1)} async-done(((bf16[64,769]{1,0:T(8,128)(2,1)}), bf16[2048,769]{1,0:T(8,128)(2,1)}) %all-gather.4.cloned.1.call-update) | async-done | bytes 3149840 | tf_op jit(solution)/shard_map/all_gather | solution.py:15
  64.3 1.4 convert_reduce_fusion
  65.7 2.0 fusion.20
  69.0 1.9 copy-done
  70.9 8.0 %fusion.49 = f32[512,512]{0,1:T(8,128)} fusion(f32[2048,512]{1,0:T(8,128)S(1)} %multiply_multiply_fusion.1), kind=kOutput, calls=%fused_computation.94 | convolution fusion | flops 6442450944 | bytes 5242880 | tf_op jit(solution)/shard_map/dot_general | solution.py:54
  79.3 2.4 fusion.18
  81.7 4.7 %multiply_multiply_fusion = f32[2048,768]{1,0:T(8,128)} fusion(f32[2048,768]{1,0:T(8,128)S(1)} %fusion.18, f32[2048]{0:T(1024)S(1)} %convert_reduce_fusion, bf16[2048,769]{1,0:T(8,128)(2,1)S(1)} %copy-done.3, s32[768]{0:T(1024)S(1)} %get-tuple-element.10), kind=kOutput, calls=%fused_computation.2 | convolution fusion | flops 1614151680 | bytes 14692352 | tf_op jit(solution)/shard_map/dot_general | solution.py:34
  86.4 68.5 %all-reduce.4.cloned.1.call-done = f32[512,512]{0,1:T(8,128)} async-done(((f32[512,512]{0,1:T(8,128)}), f32[512,512]{0,1:T(8,128)}) %all-reduce.4.cloned.1.call-update) | async-done | bytes 1048592 | tf_op jit(solution)/shard_map/psum | solution.py:57
  154.9 1.6 copy.14
  156.4 1.4 fusion.17
  157.9 11.7 %cholesky.104 = f32[128,128]{1,0:T(8,128)S(1)} custom-call(f32[128,128]{1,0:T(8,128)S(1)} %cholesky.266), custom_call_target="Cholesky" | custom-call | tf_op jit(solution)/shard_map/jit(cholesky)/cholesky | solution.py:39
  169.6 9.8 %custom-call.30 = f32[1,128,128]{1,2,0:T(8,128)S(1)} custom-call(f32[1,128,128]{2,1,0:T(8,128)S(1)} %get-tuple-element.33), custom_call_target="InvertDiagBlocksLowerTriangular" | custom-call | tf_op jit(solution)/shard_map/jit(cholesky)/cholesky | solution.py:39
  180.3 12.2 %cholesky.217 = f32[128,128]{1,0:T(8,128)S(1)} custom-call(f32[128,128]{1,0:T(8,128)S(1)} %cholesky.270), custom_call_target="Cholesky" | custom-call | tf_op jit(solution)/shard_map/jit(cholesky)/cholesky | solution.py:39
  192.4 9.8 %custom-call.31 = f32[1,128,128]{1,2,0:T(8,128)S(1)} custom-call(f32[1,128,128]{2,1,0:T(8,128)S(1)} %get-tuple-element.30), custom_call_target="InvertDiagBlocksLowerTriangular" | custom-call | tf_op jit(solution)/shard_map/jit(cholesky)/cholesky | solution.py:39
  202.9 11.7 %cholesky.238 = f32[128,128]{1,0:T(8,128)S(1)} custom-call(f32[128,128]{1,0:T(8,128)S(1)} %cholesky.275), custom_call_target="Cholesky" | custom-call | tf_op jit(solution)/shard_map/jit(cholesky)/cholesky | solution.py:39
  215.3 9.8 %custom-call.32 = f32[1,128,128]{1,2,0:T(8,128)S(1)} custom-call(f32[1,128,128]{2,1,0:T(8,128)S(1)} %get-tuple-element.27), custom_call_target="InvertDiagBlocksLowerTriangular" | custom-call | tf_op jit(solution)/shard_map/jit(cholesky)/cholesky | solution.py:39
  225.7 11.9 %cholesky.255 = f32[128,128]{1,0:T(8,128)S(1)} custom-call(f32[128,128]{1,0:T(8,128)S(1)} %convolution_subtract_fusion.5), custom_call_target="Cholesky" | custom-call | tf_op jit(solution)/shard_map/jit(cholesky)/cholesky | solution.py:39
  241.7 10.3 %while.1 = (s32[]{:T(128)}, f32[512,512]{1,0:T(8,128)S(1)}, s32[4,2]{0,1:T(2,128)S(1)}, f32[4,128,128]{2,1,0:T(8,128)}, s32[]{:T(128)}) while((s32[]{:T(128)}, f32[512,512]{1,0:T(8,128)S(1)}, s32[4,2]{0,1:T(2,128)S(1)}, f32[4,128,128]{2,1,0:T(8,128)}, s32[]{:T(128)}) %tuple.33), condition=%wide.while_cond, body=%wide.while_body.sunk | while | flops 2 | bytes 132205 | solution.py:40
  242.3 2.0 bitcast_dynamic-update-slice_fusion.2
  244.9 2.0 bitcast_dynamic-update-slice_fusion.2
  247.5 2.0 bitcast_dynamic-update-slice_fusion.2
  250.1 2.0 bitcast_dynamic-update-slice_fusion.2
  252.0 40.2 %custom-call.33 = f32[4,128,128]{1,2,0:T(8,128)S(1)} custom-call(f32[4,128,128]{2,1,0:T(8,128)} %get-tuple-element.9), custom_call_target="InvertDiagBlocksLowerTriangular" | custom-call | tf_op jit(solution)/shard_map/triangular_solve | solution.py:40
  292.2 2.4 fusion.15
  294.7 3.0 convolution_subtract_fusion.2
  298.8 3.5 convolution_subtract_fusion.1
  303.5 6.6 %fusion.6 = f32[128,2048]{0,1:T(8,128)S(1)} fusion(f32[128,2048]{1,0:T(8,128)S(1)} %fusion.35, f32[128,2048]{1,0:T(8,128)S(1)} %fusion.37, f32[128,2048]{1,0:T(8,128)S(1)} %fusion.15, f32[512,2048]{0,1:T(8,128)S(1)} %bitcast.61, f32[512,512]{1,0:T(8,128)} %copy-done.6), kind=kOutput, calls=%fused_computation.12 | convolution fusion | flops 1209794560 | bytes 5439488 | tf_op jit(solution)/shard_map/triangular_solve | solution.py:40
  312.2 11.6 %fusion.9 = f32[512,768]{1,0:T(8,128)} fusion(f32[2048,768]{1,0:T(8,128)S(1)} %bitcast.63, f32[128,2048]{1,0:T(8,128)S(1)} %fusion.34, f32[128,2048]{1,0:T(8,128)S(1)} %fusion.35, f32[128,2048]{1,0:T(8,128)S(1)} %fusion.37, f32[128,2048]{1,0:T(8,128)S(1)} %fusion.15), kind=kOutput, calls=%fused_computation.15 | convolution fusion | flops 9666822144 | bytes 12058624 | tf_op jit(solution)/shard_map/dot_general | solution.py:59
  323.8 77.3 %all-reduce.6.cloned.1.call-done = f32[512,768]{1,0:T(8,128)} async-done(((f32[512,768]{1,0:T(8,128)}), f32[512,768]{1,0:T(8,128)}) %all-reduce.6.cloned.1.call-update) | async-done | bytes 1572880 | tf_op jit(solution)/shard_map/psum | solution.py:62
  401.0 23.9 %convolution_subtract_fusion = f32[2048,768]{1,0:T(8,128)} fusion(f32[2048,768]{1,0:T(8,128)} %multiply_multiply_fusion, f32[512,768]{1,0:T(8,128)} %all-reduce.6.cloned.1.call-done, f32[128,2048]{1,0:T(8,128)} %copy-done.5, f32[128,2048]{1,0:T(8,128)S(1)} %fusion.35, f32[128,2048]{1,0:T(8,128)S(1)} %fusion.37, f32[128,2048]{1,0:T(8,128)S(1)} %fusion.15), kind=kOutput, calls=%fused_computation.5 | convolution fusion | flops 9668395008 | bytes 18350080 | tf_op jit(solution)/shard_map/dot_general | solution.py:44
  (62 shorter events, 16.0 us)
Async XLA Ops:
  7.2 57.1 %all-gather.4.cloned.1.call-start = ((), (), s32[]{:S(2)}) async-start(), calls=%async_computation | async-start | bytes 3784704 | tf_op jit(solution)/shard_map/all_gather | solution.py:15
  9.5 145.4 %all-reduce.4.cloned.1.call-start = ((), (), s32[]{:S(2)}) async-start(), calls=%async_computation.1 | async-start | bytes 2097152 | tf_op jit(solution)/shard_map/psum | solution.py:57
  64.3 3.4 copy-start.2
  69.0 1.9 copy-start
  79.0 322.0 %all-reduce.6.cloned.1.call-start = ((), (), s32[]{:S(2)}) async-start(), calls=%async_computation.2 | async-start | bytes 3145728 | tf_op jit(solution)/shard_map/psum | solution.py:62
  79.3 2.4 copy-start.3
  252.0 46.8 %copy-start.6 = (f32[512,512]{1,0:T(8,128)}, f32[512,512]{1,0:T(8,128)S(1)}, u32[]{:S(2)}) copy-start(f32[512,512]{1,0:T(8,128)S(1)} %get-tuple-element.92) | copy-start | bytes 3145732
  292.2 6.6 %copy-start.1 = (f32[2048,512]{1,0:T(8,128)S(1)}, f32[2048,512]{1,0:T(8,128)}, u32[]{:S(2)}) copy-start(f32[2048,512]{1,0:T(8,128)} %copy-done) | copy-start | bytes 12582916
  298.8 13.4 %slice-start = ((s8[6291456]{0:T(1024)(128)(4,1)}), s8[4194304]{0:T(1024)(128)(4,1)S(1)}, s32[]{:S(2)}) async-start(s8[6291456]{0:T(1024)(128)(4,1)} %bitcast.62), calls=%async_computation.3 | async-start | bytes 8388608
  303.4 8.7 %slice-start.1 = ((s8[6291456]{0:T(1024)(128)(4,1)}), s8[2097152]{0:T(1024)(128)(4,1)S(1)}, s32[]{:S(2)}) async-start(s8[6291456]{0:T(1024)(128)(4,1)} %bitcast.62), calls=%async_computation.4 | async-start | bytes 4194304
  311.2 1.0 copy-start.5
  401.0 23.9 %copy-start.4 = (f32[512,768]{1,0:T(8,128)S(1)}, f32[512,768]{1,0:T(8,128)}, u32[]{:S(2)}) copy-start(f32[512,768]{1,0:T(8,128)} %all-reduce.6.cloned.1.call-done) | copy-start | bytes 4718596
Sparse Core Ops, SparseCore 0:
  11.1 53.1 all-gather.3
  79.1 75.7 all-reduce.3
  323.9 77.1 all-reduce.5
where the time goes:
time: 441 us; the launch traced here: 433 us
  waiting for transfers between devices  174 us (39%)
  other arithmetic  124 us (28%)
  matrix products  74.6 us (17%)
  blocking collectives  24.6 us (6%)
  local copies, waits for them, and re-layouts  18.3 us (4%)
  between operations  17.1 us (4%)
    another operation x14, other arithmetic, orthonormal(): lower_factor = jnp.linalg.cholesky(gram_sum)  79 us
    psum x1, waiting for transfers between devices, shards(): coefficients = lax.psum(local_rows, 'row')  77.3 us
    psum x1, waiting for transfers between devices, shards(): gram_sum = lax.psum(local_gram, 'row')  68.5 us
    another operation x3, other arithmetic, orthonormal(): lax.linalg.triangular_solve(lower_factor, panel_cols.T, left_side=True, l...  40.3 us
    all_gather x1, waiting for transfers between devices, in_one_piece(): result = lax.all_gather(both, axis, axis=dim, tiled=True)  28.7 us
    all_gather x1, blocking collectives, picked(): lax.all_gather(array, axis)  24.6 us
    dot_general x1, matrix products, remove_span(): jnp.dot(basis_t.T, top_rows, precision=lax.Precision.HIGHEST, preferred_e...  23.9 us
    another operation x7, matrix products, orthonormal(): lax.linalg.triangular_solve(lower_factor, panel_cols.T, left_side=True, l...  18.9 us
  transfers between devices with their start and end apart: 3, of which 3 were waited for; matrix products, arithmetic and copies ran while one was open for 2% of the time, Pallas kernels for 0%

commit v1 on v0

--- a/solution.py
+++ b/solution.py
@@ -5,6 +5,14 @@
 from jax.sharding import PartitionSpec as P
 
 PANEL = 256
+
+
+def doubling_sum(array, name):
+    size, total = (lax.axis_size(name), array)
+    for hop in [1 << k for k in range(size.bit_length() - 1)]:
+        swap = [(i, i ^ hop) for i in range(size)]
+        total = total + lax.ppermute(total, name, swap)
+    return total
 
 
 def in_one_piece(arrays, axis, dim, along):
@@ -54,7 +62,7 @@
     local_gram = jnp.dot(
         lead_cols.T, lead_cols, precision=lax.Precision.HIGHEST, preferred_element_type=jnp.float32
     )
-    gram_sum = lax.psum(local_gram, "row")
+    gram_sum = doubling_sum(local_gram, "row")
     basis_t = orthonormal(lead_cols, gram_sum)
     local_rows = jnp.dot(
         basis_t, design, precision=lax.Precision.HIGHEST, preferred_element_type=jnp.float32

time: 441 us -> 486 us (1.10)
  waiting for transfers between devices: 174 us -> 213 us
  starting transfers between devices: 0.34 us -> 10.3 us
    ppermute x0 -> x3, waiting for transfers between devices: none -> 108 us  [doubling_sum(): total = total + lax.ppermute(total, name, swap)]
    psum x1 -> x0, waiting for transfers between devices: 68.5 us -> none  [shards(): gram_sum = lax.psum(local_gram, 'row')]
    ppermute x0 -> x3, starting transfers between devices: none -> 10.3 us  [doubling_sum(): total = total + lax.ppermute(total, name, swap)]
  transfers between devices with their start and end apart: 3 -> 5, of which waited for: 3 -> 5; matrix products, arithmetic and copies ran while one was open for 2% -> 2% of each run, Pallas kernels for 0% -> 0%
where the time goes in v1:
time: 486 us; the launch traced here: 477 us
  waiting for transfers between devices  213 us (44%)
  other arithmetic  123 us (25%)
  matrix products  73.6 us (15%)
  blocking collectives  24.6 us (5%)
  between operations  17.3 us (4%)
  local copies, waits for them, and re-layouts  14.3 us (3%)
  starting transfers between devices  10.3 us (2%)
    ppermute x3, waiting for transfers between devices, doubling_sum(): total = total + lax.ppermute(total, name, swap)  108 us
    another operation x14, other arithmetic, orthonormal(): lower_factor = jnp.linalg.cholesky(gram_sum)  79 us
    psum x1, waiting for transfers between devices, shards(): coefficients = lax.psum(local_rows, 'row')  75.8 us
    another operation x3, other arithmetic, orthonormal(): lax.linalg.triangular_solve(lower_factor, panel_cols.T, left_side=True, l...  40.3 us
    all_gather x1, waiting for transfers between devices, in_one_piece(): result = lax.all_gather(both, axis, axis=dim, tiled=True)  29.5 us
    all_gather x1, blocking collectives, picked(): lax.all_gather(array, axis)  24.6 us
    dot_general x1, matrix products, remove_span(): jnp.dot(basis_t.T, top_rows, precision=lax.Precision.HIGHEST, preferred_e...  23.9 us
    another operation x7, matrix products, orthonormal(): lax.linalg.triangular_solve(lower_factor, panel_cols.T, left_side=True, l...  18.9 us
  transfers between devices with their start and end apart: 5, of which 5 were waited for; matrix products, arithmetic and copies ran while one was open for 2% of the time, Pallas kernels for 0%

profile of v1, /device:TPU:2, one launch (start us, length us, event | category | flops | bytes accessed | tf_op | source)
XLA Modules:
  0.0 476.6 jit_solution(11968567038433805005)
XLA Ops:
  10.2 24.6 %all-gather.1 = s32[32,2,512]{2,1,0:T(2,128)S(1)} all-gather(s32[1,2,512]{2,1,0:T(2,128)S(1)} %slice_bitcast_fusion.8), channel_id=2, replica_groups=mesh['row'=8,'col'=32] {'col'}, dimensions={0}, use_global_device_ids=true | all-gather | bytes 135168 | tf_op jit(solution)/shard_map/all_gather | solution.py:31
  34.8 29.5 %all-gather.4.cloned.1.call-done = bf16[2048,769]{1,0:T(8,128)(2,1)} async-done(((bf16[64,769]{1,0:T(8,128)(2,1)}), bf16[2048,769]{1,0:T(8,128)(2,1)}) %all-gather.4.cloned.1.call-update) | async-done | bytes 3149840 | tf_op jit(solution)/shard_map/all_gather | solution.py:23
  65.7 2.0 fusion.20
  69.0 7.1 %fusion.54 = f32[512,512]{0,1:T(8,128)S(1)} fusion(f32[2048,512]{1,0:T(8,128)S(1)} %multiply_multiply_fusion.1), kind=kOutput, calls=%fused_computation.97 | convolution fusion | flops 6442450944 | bytes 5242880 | tf_op jit(solution)/shard_map/dot_general | solution.py:62
  76.1 1.6 collective-permute-start
  77.8 23.8 %collective-permute-done = f32[512,512]{0,1:T(8,128)S(1)} collective-permute-done((f32[512,512]{0,1:T(8,128)S(1)}, f32[512,512]{0,1:T(8,128)S(1)}, u32[]{:S(2)}, u32[]{:S(2)}) %collective-permute-start) | collective-permute-done | bytes 1048608 | tf_op jit(solution)/shard_map/ppermute | solution.py:14
  101.7 2.6 collective-permute-start.1
  104.4 45.3 %collective-permute-done.1 = f32[512,512]{0,1:T(8,128)S(1)} collective-permute-done((f32[512,512]{0,1:T(8,128)S(1)}, f32[512,512]{0,1:T(8,128)S(1)}, u32[]{:S(2)}, u32[]{:S(2)}) %collective-permute-start.1) | collective-permute-done | bytes 1048608 | tf_op jit(solution)/shard_map/ppermute | solution.py:14
  149.9 6.0 %collective-permute-start.2 = (f32[512,512]{0,1:T(8,128)S(1)}, f32[512,512]{0,1:T(8,128)S(1)}, u32[]{:S(2)}, u32[]{:S(2)}) collective-permute-start(f32[512,512]{0,1:T(8,128)S(1)} %add.54), channel_id=1, source_target_pairs={{0,128},{32,160},{64,192},{96,224},{128,0},{160,32},{192,64},{224,... | collective-permute-start | bytes 3145736 | tf_op jit(solution)/shard_map/ppermute | solution.py:14
  155.9 2.4 fusion.18
  158.3 4.7 multiply_multiply_fusion
  163.0 39.0 %collective-permute-done.2 = f32[512,512]{0,1:T(8,128)S(1)} collective-permute-done((f32[512,512]{0,1:T(8,128)S(1)}, f32[512,512]{0,1:T(8,128)S(1)}, u32[]{:S(2)}, u32[]{:S(2)}) %collective-permute-start.2) | collective-permute-done | bytes 1048608 | tf_op jit(solution)/shard_map/ppermute | solution.py:14
  202.9 11.7 %cholesky.104 = f32[128,128]{1,0:T(8,128)S(1)} custom-call(f32[128,128]{1,0:T(8,128)S(1)} %cholesky.266), custom_call_target="Cholesky" | custom-call | tf_op jit(solution)/shard_map/jit(cholesky)/cholesky | solution.py:47
  214.6 9.8 %custom-call.30 = f32[1,128,128]{1,2,0:T(8,128)S(1)} custom-call(f32[1,128,128]{2,1,0:T(8,128)S(1)} %get-tuple-element.33), custom_call_target="InvertDiagBlocksLowerTriangular" | custom-call | tf_op jit(solution)/shard_map/jit(cholesky)/cholesky | solution.py:47
  225.2 12.1 %cholesky.217 = f32[128,128]{1,0:T(8,128)S(1)} custom-call(f32[128,128]{1,0:T(8,128)S(1)} %cholesky.270), custom_call_target="Cholesky" | custom-call | tf_op jit(solution)/shard_map/jit(cholesky)/cholesky | solution.py:47
  237.3 9.8 %custom-call.31 = f32[1,128,128]{1,2,0:T(8,128)S(1)} custom-call(f32[1,128,128]{2,1,0:T(8,128)S(1)} %get-tuple-element.30), custom_call_target="InvertDiagBlocksLowerTriangular" | custom-call | tf_op jit(solution)/shard_map/jit(cholesky)/cholesky | solution.py:47
  247.8 11.7 %cholesky.238 = f32[128,128]{1,0:T(8,128)S(1)} custom-call(f32[128,128]{1,0:T(8,128)S(1)} %cholesky.275), custom_call_target="Cholesky" | custom-call | tf_op jit(solution)/shard_map/jit(cholesky)/cholesky | solution.py:47
  260.2 9.8 %custom-call.32 = f32[1,128,128]{1,2,0:T(8,128)S(1)} custom-call(f32[1,128,128]{2,1,0:T(8,128)S(1)} %get-tuple-element.27), custom_call_target="InvertDiagBlocksLowerTriangular" | custom-call | tf_op jit(solution)/shard_map/jit(cholesky)/cholesky | solution.py:47
  270.6 11.9 %cholesky.255 = f32[128,128]{1,0:T(8,128)S(1)} custom-call(f32[128,128]{1,0:T(8,128)S(1)} %slice_subtract_fusion.2), custom_call_target="Cholesky" | custom-call | tf_op jit(solution)/shard_map/jit(cholesky)/cholesky | solution.py:47
  286.6 10.2 %while.1 = (s32[]{:T(128)}, f32[512,512]{1,0:T(8,128)S(1)}, s32[4,2]{0,1:T(2,128)S(1)}, f32[4,128,128]{2,1,0:T(8,128)}, s32[]{:T(128)}) while((s32[]{:T(128)}, f32[512,512]{1,0:T(8,128)S(1)}, s32[4,2]{0,1:T(2,128)S(1)}, f32[4,128,128]{2,1,0:T(8,128)}, s32[]{:T(128)}) %tuple.33), condition=%wide.while_cond, body=%wide.while_body.sunk | while | flops 2 | bytes 132205 | solution.py:48
  287.2 1.9 bitcast_dynamic-update-slice_fusion.2
  289.7 1.9 bitcast_dynamic-update-slice_fusion.2
  292.3 1.9 bitcast_dynamic-update-slice_fusion.2
  294.9 1.9 bitcast_dynamic-update-slice_fusion.2
  296.8 40.2 %custom-call.33 = f32[4,128,128]{1,2,0:T(8,128)S(1)} custom-call(f32[4,128,128]{2,1,0:T(8,128)} %get-tuple-element.9), custom_call_target="InvertDiagBlocksLowerTriangular" | custom-call | tf_op jit(solution)/shard_map/triangular_solve | solution.py:48
  337.0 2.4 fusion.15
  339.4 3.0 convolution_subtract_fusion.2
  343.6 3.5 convolution_subtract_fusion.1
  348.2 6.6 %fusion.6 = f32[128,2048]{0,1:T(8,128)S(1)} fusion(f32[128,2048]{1,0:T(8,128)S(1)} %fusion.37, f32[128,2048]{1,0:T(8,128)S(1)} %fusion.39, f32[128,2048]{1,0:T(8,128)S(1)} %fusion.15, f32[512,2048]{0,1:T(8,128)S(1)} %bitcast.61, f32[512,512]{1,0:T(8,128)} %copy-done.6), kind=kOutput, calls=%fused_computation.12 | convolution fusion | flops 1209794560 | bytes 5439488 | tf_op jit(solution)/shard_map/triangular_solve | solution.py:48
  356.9 11.6 %fusion.9 = f32[512,768]{1,0:T(8,128)} fusion(f32[2048,768]{1,0:T(8,128)S(1)} %bitcast.63, f32[128,2048]{1,0:T(8,128)S(1)} %fusion.36, f32[128,2048]{1,0:T(8,128)S(1)} %fusion.37, f32[128,2048]{1,0:T(8,128)S(1)} %fusion.39, f32[128,2048]{1,0:T(8,128)S(1)} %fusion.15), kind=kOutput, calls=%fused_computation.15 | convolution fusion | flops 9666822144 | bytes 12058624 | tf_op jit(solution)/shard_map/dot_general | solution.py:67
  368.5 75.8 %all-reduce.3.cloned.1.call-done = f32[512,768]{1,0:T(8,128)} async-done(((f32[512,768]{1,0:T(8,128)}), f32[512,768]{1,0:T(8,128)}) %all-reduce.3.cloned.1.call-update) | async-done | bytes 1572880 | tf_op jit(solution)/shard_map/psum | solution.py:70
  444.3 23.9 %convolution_subtract_fusion = f32[2048,768]{1,0:T(8,128)} fusion(f32[2048,768]{1,0:T(8,128)} %multiply_multiply_fusion, f32[512,768]{1,0:T(8,128)} %all-reduce.3.cloned.1.call-done, f32[128,2048]{1,0:T(8,128)} %copy-done.5, f32[128,2048]{1,0:T(8,128)S(1)} %fusion.37, f32[128,2048]{1,0:T(8,128)S(1)} %fusion.39, f32[128,2048]{1,0:T(8,128)S(1)} %fusion.15), kind=kOutput, calls=%fused_computation.5 | convolution fusion | flops 9668395008 | bytes 18350080 | tf_op jit(solution)/shard_map/dot_general | solution.py:52
  (70 shorter events, 19.1 us)
Async XLA Ops:
  7.2 57.1 %all-gather.4.cloned.1.call-start = ((), (), s32[]{:S(2)}) async-start(), calls=%async_computation | async-start | bytes 3784704 | tf_op jit(solution)/shard_map/all_gather | solution.py:23
  9.5 434.8 %all-reduce.3.cloned.1.call-start = ((), (), s32[]{:S(2)}) async-start(), calls=%async_computation.1 | async-start | bytes 3145728 | tf_op jit(solution)/shard_map/psum | solution.py:70
  64.3 3.4 copy-start.2
  69.0 7.1 %copy-start = (f32[2048,512]{1,0:T(8,128)}, f32[2048,512]{1,0:T(8,128)S(1)}, u32[]{:S(2)}) copy-start(f32[2048,512]{1,0:T(8,128)S(1)} %multiply_multiply_fusion.1) | copy-start | bytes 12582916
  69.0 35.3 %copy-start.7 = (s32[2,768]{1,0:T(2,128)S(1)}, s32[2,768]{1,0:T(2,128)}, u32[]{:S(2)}) copy-start(s32[2,768]{1,0:T(2,128)} %param.7) | copy-start | bytes 18436
  76.1 25.4 %collective-permute-start = (f32[512,512]{0,1:T(8,128)S(1)}, f32[512,512]{0,1:T(8,128)S(1)}, u32[]{:S(2)}, u32[]{:S(2)}) collective-permute-start(f32[512,512]{0,1:T(8,128)S(1)} %fusion.54), channel_id=1, source_target_pairs={{0,32},{32,0},{64,96},{96,64},{128,160},{160,128},{192,224},{224,1... | collective-permute-start | bytes 3145736 | tf_op jit(solution)/shard_map/ppermute | solution.py:14
  101.7 48.0 %collective-permute-start.1 = (f32[512,512]{0,1:T(8,128)S(1)}, f32[512,512]{0,1:T(8,128)S(1)}, u32[]{:S(2)}, u32[]{:S(2)}) collective-permute-start(f32[512,512]{0,1:T(8,128)S(1)} %add.53), channel_id=1, source_target_pairs={{0,64},{32,96},{64,0},{96,32},{128,192},{160,224},{192,128},{224,1... | collective-permute-start | bytes 3145736 | tf_op jit(solution)/shard_map/ppermute | solution.py:14
  149.9 52.2 %collective-permute-start.2 = (f32[512,512]{0,1:T(8,128)S(1)}, f32[512,512]{0,1:T(8,128)S(1)}, u32[]{:S(2)}, u32[]{:S(2)}) collective-permute-start(f32[512,512]{0,1:T(8,128)S(1)} %add.54), channel_id=1, source_target_pairs={{0,128},{32,160},{64,192},{96,224},{128,0},{160,32},{192,64},{224,... | collective-permute-start | bytes 3145736 | tf_op jit(solution)/shard_map/ppermute | solution.py:14
  155.9 2.4 copy-start.3
  296.8 46.7 %copy-start.6 = (f32[512,512]{1,0:T(8,128)}, f32[512,512]{1,0:T(8,128)S(1)}, u32[]{:S(2)}) copy-start(f32[512,512]{1,0:T(8,128)S(1)} %get-tuple-element.91) | copy-start | bytes 3145732
  337.0 6.6 %copy-start.1 = (f32[2048,512]{1,0:T(8,128)S(1)}, f32[2048,512]{1,0:T(8,128)}, u32[]{:S(2)}) copy-start(f32[2048,512]{1,0:T(8,128)} %copy-done) | copy-start | bytes 12582916
  343.6 13.4 %slice-start = ((s8[6291456]{0:T(1024)(128)(4,1)}), s8[4194304]{0:T(1024)(128)(4,1)S(1)}, s32[]{:S(2)}) async-start(s8[6291456]{0:T(1024)(128)(4,1)} %bitcast.62), calls=%async_computation.2 | async-start | bytes 8388608
  348.2 8.7 %slice-start.1 = ((s8[6291456]{0:T(1024)(128)(4,1)}), s8[2097152]{0:T(1024)(128)(4,1)S(1)}, s32[]{:S(2)}) async-start(s8[6291456]{0:T(1024)(128)(4,1)} %bitcast.62), calls=%async_computation.3 | async-start | bytes 4194304
  355.9 1.0 copy-start.5
  444.3 23.9 %copy-start.4 = (f32[512,768]{1,0:T(8,128)S(1)}, f32[512,768]{1,0:T(8,128)}, u32[]{:S(2)}) copy-start(f32[512,768]{1,0:T(8,128)} %all-reduce.3.cloned.1.call-done) | copy-start | bytes 4718596
Sparse Core Ops, SparseCore 0:
  11.1 53.1 all-gather.3
  368.6 75.5 all-reduce.2
